TPU v7x, 32 devices: a whole 2x2x4 slice. The times are simulated.
32 devices in a mesh: wide: 8 (over z, x), narrow: 4 (over y, core).
Axes of the slice: x: 2, y: 2, z: 4, core: 2. Of those that a mesh axis runs over, the one named last changes fastest.
Arguments:
- tokens_in: bfloat16 [8192, 2048], P(('wide', 'narrow')), may hold values from -6 to 6
- segment_starts: int32 [8192], P(('wide', 'narrow')), may hold values 0 or 1
- cotangent: bfloat16 [8192, 2048], P(('wide', 'narrow')), may hold values from -6 to 6
- norm1_gain: bfloat16 [2048], P(('wide', 'narrow')), may hold values from 0.25 to 1.75
- rec_gate_weight: bfloat16 [2048, 2560], P(('wide', 'narrow')), may hold values from -0.125 to 0.125
- rec_in_weight: bfloat16 [2048, 2560], P(('wide', 'narrow')), may hold values from -0.125 to 0.125
- conv_weight: bfloat16 [2560, 4], P(('wide', 'narrow')), may hold values from -3 to 3
- conv_bias: bfloat16 [2560], P(('wide', 'narrow')), may hold values from -3 to 3
- gate_a_weight: bfloat16 [2560, 160], P(('wide', 'narrow')), may hold values from -0.5 to 0.5
- gate_a_bias: bfloat16 [2560], P(('wide', 'narrow')), may hold values from -4 to 4
- gate_x_weight: bfloat16 [2560, 160], P(('wide', 'narrow')), may hold values from -0.5 to 0.5
- gate_x_bias: bfloat16 [2560], P(('wide', 'narrow')), may hold values from -4 to 4
- decay_rate: bfloat16 [2560], P(('wide', 'narrow')), may hold values from 7.772446e-05 to 0.049804688
- rec_out_weight: bfloat16 [2560, 2048], P(('wide', 'narrow')), may hold values from -0.125 to 0.125
- norm2_gain: bfloat16 [2048], P(('wide', 'narrow')), may hold values from 0.25 to 1.75
- mlp_gate_weight: bfloat16 [2048, 6144], P(('wide', 'narrow')), may hold values from -0.125 to 0.125
- mlp_up_weight: bfloat16 [2048, 6144], P(('wide', 'narrow')), may hold values from -0.125 to 0.125
- mlp_down_weight: bfloat16 [6144, 2048], P(('wide', 'narrow')), may hold values from -0.078125 to 0.078125
Outputs:
- layer_out: bfloat16 [8192, 2048], P(('wide', 'narrow'))
- grad_tokens: float32 [8192, 2048], P(('wide', 'narrow'))
- grad_norm1_gain: float32 [2048], P(('wide', 'narrow'))
- grad_rec_gate_weight: float32 [2048, 2560], P(('wide', 'narrow'))
- grad_rec_in_weight: float32 [2048, 2560], P(('wide', 'narrow'))
- grad_conv_weight: float32 [2560, 4], P(('wide', 'narrow'))
- grad_conv_bias: float32 [2560], P(('wide', 'narrow'))
- grad_gate_a_weight: float32 [2560, 160], P(('wide', 'narrow'))
- grad_gate_a_bias: float32 [2560], P(('wide', 'narrow'))
- grad_gate_x_weight: float32 [2560, 160], P(('wide', 'narrow'))
- grad_gate_x_bias: float32 [2560], P(('wide', 'narrow'))
- grad_decay_rate: float32 [2560], P(('wide', 'narrow'))
- grad_rec_out_weight: float32 [2560, 2048], P(('wide', 'narrow'))
- grad_norm2_gain: float32 [2048], P(('wide', 'narrow'))
- grad_mlp_gate_weight: float32 [2048, 6144], P(('wide', 'narrow'))
- grad_mlp_up_weight: float32 [2048, 6144], P(('wide', 'narrow'))
- grad_mlp_down_weight: float32 [6144, 2048], P(('wide', 'narrow'))
Inputs may be any that keep to these rules, and one draw needn't show every extreme that they name: `segment_starts`: documents run on across the boundaries between devices.
All inputs are finite; a program needn't handle non-finite values.
Results may differ from a plain program's by a relative error of at most 0.011.
Values may be sent and summed in bfloat16 or wider, within the bound.
A program may use at most 512 MiB of HBM per device.

v0:
```python
import jax
import jax.numpy as jnp
from jax import lax
from jax.sharding import PartitionSpec as P

NB = 16
BLK = 160
CONV = 4
norm_eps = 1e-06
decay_scale = 8.0
push_shift = 0.05
contract_last = (((1,), (1,)), ((), ()))
contract_first = (((0,), (0,)), ((), ()))


def shifted(block, axis, distance):
    devices = range(lax.axis_size(axis))
    route = [(i - distance, i) for i in devices if i - distance in devices]
    return lax.ppermute(block, axis, route)


def carried_in(part, axis, combine, identity, reverse):
    count = lax.axis_size(axis)
    place = lax.axis_index(axis)
    ahead = count - 1 - place if reverse else place
    gathered = jax.tree.map(lambda a: lax.all_gather(a, axis), part)
    state = jax.tree.map(lambda a, e: jnp.zeros_like(a) + jnp.asarray(e, a.dtype), part, identity)

    def one(hop, state):
        source = count - 1 - hop if reverse else hop
        return combine(
            state, jax.tree.map(lambda a: lax.dynamic_index_in_dim(a, source, 0, False), gathered)
        )

    return lax.fori_loop(0, ahead, one, state)


def rms_scale(tok_rows, gain):
    return (
        tok_rows
        * lax.rsqrt(jnp.mean(tok_rows * tok_rows, axis=-1, keepdims=True) + norm_eps)
        * gain
    )


def gelu_tanh(values):
    return jax.nn.gelu(values, approximate=True)


def gated_unit(gate_vals, up_vals):
    return gelu_tanh(gate_vals) * up_vals


def combine_pairs(earlier, later):
    return (earlier[0] * later[0], later[0] * earlier[1] + later[1])


def conv_apply(extended, conv_taps, conv_offset, ids_ext, seg_local):
    row_total = seg_local.shape[0]
    tap_total = conv_taps.shape[1]
    summed = jnp.zeros((row_total, conv_taps.shape[0]), jnp.float32) + conv_offset
    for tap_index in range(tap_total):
        begin = tap_total - 1 - tap_index
        window = extended[begin : begin + row_total]
        same_doc = (ids_ext[begin : begin + row_total] == seg_local).astype(jnp.float32)
        summed = summed + conv_taps[:, tap_index] * window * same_doc[:, None]
    return summed


def gate_math(logit_a, logit_b, conved, rates, open_mask):
    gate_a = jax.nn.sigmoid(logit_a)
    gate_x = jax.nn.sigmoid(logit_b)
    decay = jnp.exp(-decay_scale * gate_a * rates)
    keep_all = decay * open_mask
    push_all = jnp.sqrt(1.0 - decay * decay + push_shift) * gate_x * conved
    return (keep_all, push_all)


def on_device(
    tokens_in,
    segment_starts,
    cotangent,
    norm1_gain,
    rec_gate_weight,
    rec_in_weight,
    conv_weight,
    conv_bias,
    gate_a_weight,
    gate_a_bias,
    gate_x_weight,
    gate_x_bias,
    decay_rate,
    rec_out_weight,
    norm2_gain,
    mlp_gate_weight,
    mlp_up_weight,
    mlp_down_weight,
):
    block_set = (
        lax.all_gather(norm1_gain, ("wide", "narrow"), axis=0, tiled=True),
        lax.all_gather(rec_gate_weight, ("wide", "narrow"), axis=0, tiled=True),
        lax.all_gather(rec_in_weight, ("wide", "narrow"), axis=0, tiled=True),
        lax.all_gather(conv_weight, ("wide", "narrow"), axis=0, tiled=True),
        lax.all_gather(conv_bias, ("wide", "narrow"), axis=0, tiled=True),
        lax.all_gather(gate_a_weight, ("wide", "narrow"), axis=0, tiled=True),
        lax.all_gather(gate_a_bias, ("wide", "narrow"), axis=0, tiled=True),
        lax.all_gather(gate_x_weight, ("wide", "narrow"), axis=0, tiled=True),
        lax.all_gather(gate_x_bias, ("wide", "narrow"), axis=0, tiled=True),
        lax.all_gather(decay_rate, ("wide", "narrow"), axis=0, tiled=True),
        lax.all_gather(rec_out_weight, ("wide", "narrow"), axis=0, tiled=True),
    )
    mlp_set = (
        lax.all_gather(norm2_gain, ("wide", "narrow"), axis=0, tiled=True),
        lax.all_gather(mlp_gate_weight, ("wide", "narrow"), axis=0, tiled=True),
        lax.all_gather(mlp_up_weight, ("wide", "narrow"), axis=0, tiled=True),
        lax.all_gather(mlp_down_weight, ("wide", "narrow"), axis=0, tiled=True),
    )
    (
        gain_first,
        gate_whole,
        branch_whole,
        conv_taps,
        conv_offset,
        decay_whole,
        decay_bias,
        input_whole,
        input_bias,
        decay_rates,
        output_whole,
    ) = block_set
    gain_second, mlp_gate_whole, mlp_up_whole, mlp_down_whole = mlp_set
    decay_blocks = decay_whole.reshape(NB, BLK, BLK)
    input_blocks = input_whole.reshape(NB, BLK, BLK)
    width_ff = mlp_gate_whole.shape[1]
    tok_rows = tokens_in.astype(jnp.float32)
    row_total = tok_rows.shape[0]
    tail_len = CONV - 1
    seg_local = jnp.cumsum(segment_starts)
    open_mask = (1 - segment_starts).astype(jnp.float32)[:, None]
    later_open = (seg_local[row_total - tail_len :] == seg_local[row_total - 1]).astype(
        jnp.float32
    )[:, None]
    ids_ext = jnp.concatenate([jnp.zeros((tail_len,), jnp.int32), seg_local])
    normed_f, norm_first_back = jax.vjp(rms_scale, tok_rows, gain_first.astype(jnp.float32))
    normed = normed_f.astype(jnp.bfloat16)
    gate_pre = jnp.dot(normed, gate_whole, preferred_element_type=jnp.float32)
    branch_in = jnp.dot(normed, branch_whole, preferred_element_type=jnp.float32).astype(
        jnp.bfloat16
    )
    sent_rows = branch_in[row_total - tail_len :] * later_open.astype(jnp.bfloat16)
    prev_rows = shifted(sent_rows, ("wide", "narrow"), 1)
    extended = jnp.concatenate([prev_rows, branch_in], axis=0).astype(jnp.float32)

    def conv_local(ext_rows, taps_f, offset_f):
        return conv_apply(ext_rows, taps_f, offset_f, ids_ext, seg_local)

    conv_out, conv_back = jax.vjp(
        conv_local, extended, conv_taps.astype(jnp.float32), conv_offset.astype(jnp.float32)
    )
    conved = conv_out.astype(jnp.bfloat16)
    conved_blocks = conved.reshape(row_total, NB, BLK)
    logit_a = jnp.einsum(
        "tnb,nbc->tnc", conved_blocks, decay_blocks, preferred_element_type=jnp.float32
    ).reshape(row_total, -1) + decay_bias.astype(jnp.float32)
    logit_b = jnp.einsum(
        "tnb,nbc->tnc", conved_blocks, input_blocks, preferred_element_type=jnp.float32
    ).reshape(row_total, -1) + input_bias.astype(jnp.float32)

    def gate_local(logit_one, logit_two, conved_f, rates_f):
        return gate_math(logit_one, logit_two, conved_f, rates_f, open_mask)

    (keep_all, push_all), gate_back = jax.vjp(
        gate_local, logit_a, logit_b, conved.astype(jnp.float32), decay_rates.astype(jnp.float32)
    )
    keep_prod, local_state = lax.associative_scan(combine_pairs, (keep_all, push_all), axis=0)
    ones_row = jnp.ones_like(keep_all[0])
    zeros_row = jnp.zeros_like(keep_all[0])
    prefix = carried_in(
        (keep_prod[row_total - 1], local_state[row_total - 1]),
        ("wide", "narrow"),
        combine_pairs,
        (ones_row, zeros_row),
        False,
    )
    state_in = prefix[1]
    state_all = keep_prod * state_in + local_state
    gate_act, gelu_back = jax.vjp(gelu_tanh, gate_pre)
    mixed = (state_all * gate_act).astype(jnp.bfloat16)
    middle = tok_rows + jnp.dot(mixed, output_whole, preferred_element_type=jnp.float32)
    normed_second_f, norm_second_back = jax.vjp(rms_scale, middle, gain_second.astype(jnp.float32))
    normed_two = normed_second_f.astype(jnp.bfloat16)
    mlp_gate = jnp.dot(normed_two, mlp_gate_whole, preferred_element_type=jnp.float32)
    mlp_up = jnp.dot(normed_two, mlp_up_whole, preferred_element_type=jnp.float32)
    hidden_f, mlp_back = jax.vjp(gated_unit, mlp_gate, mlp_up)
    hidden = hidden_f.astype(jnp.bfloat16)
    layer_out = (
        middle + jnp.dot(hidden, mlp_down_whole, preferred_element_type=jnp.float32)
    ).astype(jnp.bfloat16)
    d_hidden = lax.dot_general(
        cotangent, mlp_down_whole, contract_last, preferred_element_type=jnp.float32
    )
    d_mlp_gate, d_mlp_up = mlp_back(d_hidden)
    d_mlp_gate = d_mlp_gate.astype(jnp.bfloat16)
    d_mlp_up = d_mlp_up.astype(jnp.bfloat16)
    d_normed_two = lax.dot_general(
        d_mlp_gate, mlp_gate_whole, contract_last, preferred_element_type=jnp.float32
    ) + lax.dot_general(d_mlp_up, mlp_up_whole, contract_last, preferred_element_type=jnp.float32)
    d_middle_norm, d_gain_second = norm_second_back(d_normed_two)
    d_middle = cotangent.astype(jnp.float32) + d_middle_norm
    d_rec_out = d_middle.astype(jnp.bfloat16)
    d_mixed = lax.dot_general(
        d_rec_out, output_whole, contract_last, preferred_element_type=jnp.float32
    )
    (d_gate_pre,) = gelu_back(d_mixed * state_all)
    d_gate_pre = d_gate_pre.astype(jnp.bfloat16)
    d_state = d_mixed * gate_act
    keep_next = jnp.concatenate([keep_all[1:], ones_row[None]], axis=0)
    back_prod, back_local = lax.associative_scan(
        combine_pairs, (keep_next, d_state), axis=0, reverse=True
    )
    suffix = carried_in(
        (keep_prod[row_total - 1], keep_all[0] * back_local[0]),
        ("wide", "narrow"),
        combine_pairs,
        (ones_row, zeros_row),
        True,
    )
    adjoint = back_local + back_prod * suffix[1]
    state_prev = jnp.concatenate([state_in[None], state_all[: row_total - 1]], axis=0)
    d_logit_a, d_logit_b, d_conved_gate, d_rates = gate_back((adjoint * state_prev, adjoint))
    d_logit_a = d_logit_a.astype(jnp.bfloat16)
    d_logit_b = d_logit_b.astype(jnp.bfloat16)
    grad_a_blocks = d_logit_a.reshape(row_total, NB, BLK)
    grad_b_blocks = d_logit_b.reshape(row_total, NB, BLK)
    d_conved = (
        d_conved_gate
        + jnp.einsum(
            "tnc,nbc->tnb", grad_a_blocks, decay_blocks, preferred_element_type=jnp.float32
        ).reshape(row_total, -1)
        + jnp.einsum(
            "tnc,nbc->tnb", grad_b_blocks, input_blocks, preferred_element_type=jnp.float32
        ).reshape(row_total, -1)
    )
    d_conved = d_conved.astype(jnp.bfloat16)
    grad_decay_whole = jnp.einsum(
        "tnb,tnc->nbc", conved_blocks, grad_a_blocks, preferred_element_type=jnp.float32
    ).reshape(-1, BLK)
    grad_input_whole = jnp.einsum(
        "tnb,tnc->nbc", conved_blocks, grad_b_blocks, preferred_element_type=jnp.float32
    ).reshape(-1, BLK)
    grad_decay_bias = jnp.sum(d_logit_a.astype(jnp.float32), axis=0)
    grad_input_bias = jnp.sum(d_logit_b.astype(jnp.float32), axis=0)
    d_extended, d_taps, d_offset = conv_back(d_conved.astype(jnp.float32))
    from_next = shifted(d_extended[:tail_len], ("wide", "narrow"), -1)
    d_branch = d_extended[tail_len:]
    d_branch = jnp.concatenate(
        [
            d_branch[: row_total - tail_len],
            d_branch[row_total - tail_len :] + from_next * later_open,
        ],
        axis=0,
    ).astype(jnp.bfloat16)
    d_normed = lax.dot_general(
        d_gate_pre, gate_whole, contract_last, preferred_element_type=jnp.float32
    ) + lax.dot_general(d_branch, branch_whole, contract_last, preferred_element_type=jnp.float32)
    d_rows_norm, d_gain_first = norm_first_back(d_normed)
    grad_tokens = d_middle + d_rows_norm
    columns = normed
    rec_in_sum = lax.psum_scatter(
        jnp.concatenate(
            [
                lax.dot_general(
                    columns, d_gate_pre, contract_first, preferred_element_type=jnp.float32
                ),
                lax.dot_general(
                    columns, d_branch, contract_first, preferred_element_type=jnp.float32
                ),
            ],
            axis=1,
        ),
        ("wide", "narrow"),
        scatter_dimension=0,
        tiled=True,
    )
    width_rnn = gate_pre.shape[1]
    columns = mixed
    grad_output = lax.psum_scatter(
        lax.dot_general(columns, d_rec_out, contract_first, preferred_element_type=jnp.float32),
        ("wide", "narrow"),
        scatter_dimension=0,
        tiled=True,
    )
    small_sums = (
        lax.psum_scatter(d_gain_first, ("wide", "narrow"), scatter_dimension=0, tiled=True),
        lax.psum_scatter(d_taps, ("wide", "narrow"), scatter_dimension=0, tiled=True),
        lax.psum_scatter(d_offset, ("wide", "narrow"), scatter_dimension=0, tiled=True),
        lax.psum_scatter(grad_decay_whole, ("wide", "narrow"), scatter_dimension=0, tiled=True),
        lax.psum_scatter(grad_decay_bias, ("wide", "narrow"), scatter_dimension=0, tiled=True),
        lax.psum_scatter(grad_input_whole, ("wide", "narrow"), scatter_dimension=0, tiled=True),
        lax.psum_scatter(grad_input_bias, ("wide", "narrow"), scatter_dimension=0, tiled=True),
        lax.psum_scatter(d_rates, ("wide", "narrow"), scatter_dimension=0, tiled=True),
        lax.psum_scatter(d_gain_second, ("wide", "narrow"), scatter_dimension=0, tiled=True),
    )
    columns = normed_two
    mlp_in_sum = lax.psum_scatter(
        jnp.concatenate(
            [
                lax.dot_general(
                    columns, d_mlp_gate, contract_first, preferred_element_type=jnp.float32
                ),
                lax.dot_general(
                    columns, d_mlp_up, contract_first, preferred_element_type=jnp.float32
                ),
            ],
            axis=1,
        ),
        ("wide", "narrow"),
        scatter_dimension=0,
        tiled=True,
    )
    grad_gate_mlp = mlp_in_sum[:, :width_ff]
    grad_up_mlp = mlp_in_sum[:, width_ff:]
    columns = hidden
    grad_down = lax.psum_scatter(
        lax.dot_general(columns, cotangent, contract_first, preferred_element_type=jnp.float32),
        ("wide", "narrow"),
        scatter_dimension=0,
        tiled=True,
    )
    return (
        layer_out,
        grad_tokens,
        small_sums[0],
        rec_in_sum[:, :width_rnn],
        rec_in_sum[:, width_rnn:],
        small_sums[1],
        small_sums[2],
        small_sums[3],
        small_sums[4],
        small_sums[5],
        small_sums[6],
        small_sums[7],
        grad_output,
        small_sums[8],
        grad_gate_mlp,
        grad_up_mlp,
        grad_down,
    )


def solution(mesh):
    placed = (
        P(("wide", "narrow"), None),
        P(("wide", "narrow")),
        P(("wide", "narrow"), None),
        P(("wide", "narrow")),
        P(("wide", "narrow"), None),
        P(("wide", "narrow"), None),
        P(("wide", "narrow"), None),
        P(("wide", "narrow")),
        P(("wide", "narrow"), None),
        P(("wide", "narrow")),
        P(("wide", "narrow"), None),
        P(("wide", "narrow")),
        P(("wide", "narrow")),
        P(("wide", "narrow"), None),
        P(("wide", "narrow")),
        P(("wide", "narrow"), None),
        P(("wide", "narrow"), None),
        P(("wide", "narrow"), None),
    )
    return jax.shard_map(
        on_device,
        mesh=mesh,
        in_specs=placed,
        out_specs=(
            P(("wide", "narrow"), None),
            P(("wide", "narrow"), None),
            P(("wide", "narrow")),
            P(("wide", "narrow"), None),
            P(("wide", "narrow"), None),
            P(("wide", "narrow"), None),
            P(("wide", "narrow")),
            P(("wide", "narrow"), None),
            P(("wide", "narrow")),
            P(("wide", "narrow"), None),
            P(("wide", "narrow")),
            P(("wide", "narrow")),
            P(("wide", "narrow"), None),
            P(("wide", "narrow")),
            P(("wide", "narrow"), None),
            P(("wide", "narrow"), None),
            P(("wide", "narrow"), None),
        ),
        check_vma=False,
    )
```

profile of v0, /device:TPU:0, one launch (start us, length us, event | category | flops | bytes accessed | tf_op | source)
XLA Modules:
  0.0 3457.8 jit_solution(17659499854136740295)
XLA Ops:
  14.0 43.1 %all-reduce.88 = (bf16[2048]{0:T(1024)(128)(2,1)S(1)}, bf16[2560]{0:T(1024)(128)(2,1)S(1)}, bf16[2560]{0:T(1024)(128)(2,1)S(1)}, bf16[2560]{0:T(1024)(128)(2,1)S...) all-reduce(bf16[2048]{0:T(1024)(128)(2,1)S(1)} %dynamic-update-slic, ...), channel_id=1, replica_groups=mesh['wide'=8,'narrow'=4] {'wide','narrow'}, use_global_device_ids=true, to_apply=%add.76 | all-reduce | flops 14336 | bytes 57344
  57.2 40.7 %all-gather = bf16[32,80,4]{1,2,0:T(4,128)(2,1)S(1)} all-gather(bf16[1,80,4]{1,2,0:T(4,128)(2,1)S(1)} %bitcast.106), channel_id=1, replica_groups=mesh['wide'=8,'narrow'=4] {'wide','narrow'}, dimensions={0}, use_global_device_ids=true | all-gather | bytes 21120 | tf_op jit(solution)/shard_map/all_gather | solution.py:103
  100.3 46.2 %all_gather.60 = bf16[2560,160]{1,0:T(8,128)(2,1)} all-gather(bf16[80,160]{1,0:T(8,128)(2,1)S(1)} %copy-done.101), channel_id=1, replica_groups=mesh['wide'=8,'narrow'=4] {'wide','narrow'}, dimensions={0}, use_global_device_ids=true | all-gather | bytes 844800 | tf_op jit(solution)/shard_map/all_gather | solution.py:105
  146.5 48.0 %all_gather.64 = bf16[2560,160]{1,0:T(8,128)(2,1)} all-gather(bf16[80,160]{1,0:T(8,128)(2,1)S(1)} %copy-done.102), channel_id=1, replica_groups=mesh['wide'=8,'narrow'=4] {'wide','narrow'}, dimensions={0}, use_global_device_ids=true | all-gather | bytes 844800 | tf_op jit(solution)/shard_map/all_gather | solution.py:107
  363.3 41.9 %all-gather.1 = f32[32,1,2560]{2,1,0:T(1,128)S(1)} all-gather(f32[1,1,2560]{2,1,0:T(1,128)S(1)} %add_bitcast_fusion.1), channel_id=1, replica_groups=mesh['wide'=8,'narrow'=4] {'wide','narrow'}, dimensions={0}, use_global_device_ids=true | all-gather | bytes 337920 | tf_op jit(solution)/shard_map/all_gather | solution.py:26
  422.6 38.3 %all-gather.2 = f32[32,1,2560]{2,1,0:T(1,128)S(1)} all-gather(f32[1,1,2560]{2,1,0:T(1,128)S(1)} %add_bitcast_fusion), channel_id=1, replica_groups=mesh['wide'=8,'narrow'=4] {'wide','narrow'}, dimensions={0}, use_global_device_ids=true | all-gather | bytes 337920 | tf_op jit(solution)/shard_map/all_gather | solution.py:26
  524.6 79.6 %all-gather.17.cloned.1.call-done = bf16[2048,6144]{1,0:T(8,128)(2,1)} async-done(((bf16[64,6144]{1,0:T(8,128)(2,1)}), bf16[2048,6144]{1,0:T(8,128)(2,1)}) %all-gather.17.cloned.1.call-update) | async-done | bytes 25165840 | tf_op jit(solution)/shard_map/all_gather | solution.py:114
  618.5 141.3 %all-gather.21.cloned.1.call-done = bf16[6144,2048]{1,0:T(8,128)(2,1)} async-done(((bf16[192,2048]{1,0:T(8,128)(2,1)}), bf16[6144,2048]{1,0:T(8,128)(2,1)}) %all-gather.21.cloned.1.call-update) | async-done | bytes 25165840 | tf_op jit(solution)/shard_map/all_gather | solution.py:116
  759.8 21.9 multiply_convert_fusion
  946.1 39.4 %all-gather.3 = f32[32,1,2560]{2,1,0:T(1,128)S(1)} all-gather(f32[1,1,2560]{2,1,0:T(1,128)S(1)} %fusion.69), channel_id=1, replica_groups=mesh['wide'=8,'narrow'=4] {'wide','narrow'}, dimensions={0}, use_global_device_ids=true | all-gather | bytes 337920 | tf_op jit(solution)/shard_map/all_gather | solution.py:26
  985.5 30.6 while.27
  1033.2 21.0 rev.9
  1122.9 27.8 pad_maximum_fusion.1
  1151.9 21.3 fusion.110
  1173.2 21.4 fusion.109
  1194.6 66.7 %pad_maximum_fusion = f32[2048,12288]{1,0:T(8,128)} fusion(f32[2048,6144]{1,0:T(8,128)} %fusion.110, f32[2048,6144]{1,0:T(8,128)} %fusion.109), kind=kLoop, calls=%fused_computation.6 | loop fusion | flops 25165824 | bytes 201326592 | tf_op jit(solution)/shard_map/concatenate | solution.py:306
  1281.6 21.8 fusion.111
  1331.7 47.0 %all-reduce.87 = (f32[2048]{0:T(1024)S(1)}, f32[2560]{0:T(1024)S(1)}, f32[2560]{0:T(1024)S(1)}, f32[2560]{0:T(1024)S(1)}, f32[2560]{0:T(1024)S(1)}, /*index=5*/f32[2048]{0:T(1024)S(1)}) all-reduce(f32[2048]{0:T(1024)S(1)} %get-tuple-element.153, ...), channel_id=2, replica_groups=mesh['wide'=8,'narrow'=4] {'wide','narrow'}, use_global_device_ids=true, to_apply=%region_11.12.clone | all-reduce | flops 14336 | bytes 114688
  1387.1 282.5 %reduce-scatter.10.cloned.1.call-done = f32[64,5120]{1,0:T(8,128)} async-done(((f32[2048,5120]{1,0:T(8,128)}), f32[64,5120]{1,0:T(8,128)}) %reduce-scatter.10.cloned.1.call-update) | async-done | bytes 1310736 | tf_op jit(solution)/shard_map/reduce_scatter | solution.py:269
  1672.1 836.6 %reduce-scatter.18.cloned.1.call-done = f32[64,12288]{1,0:T(8,128)} async-done(((f32[2048,12288]{1,0:T(8,128)}), f32[64,12288]{1,0:T(8,128)}) %reduce-scatter.18.cloned.1.call-update) | async-done | bytes 3145744 | tf_op jit(solution)/shard_map/reduce_scatter | solution.py:305
  2512.5 135.8 %reduce-scatter.12.cloned.1.call-done = f32[80,160]{1,0:T(8,128)} async-done(((f32[2560,160]{1,0:T(8,128)}), f32[80,160]{1,0:T(8,128)}) %reduce-scatter.12.cloned.1.call-update) | async-done | bytes 51216 | tf_op jit(solution)/shard_map/reduce_scatter | solution.py:297
  2648.3 136.4 %reduce-scatter.14.cloned.1.call-done = f32[80,160]{1,0:T(8,128)} async-done(((f32[2560,160]{1,0:T(8,128)}), f32[80,160]{1,0:T(8,128)}) %reduce-scatter.14.cloned.1.call-update) | async-done | bytes 51216 | tf_op jit(solution)/shard_map/reduce_scatter | solution.py:299
  2784.7 223.8 %reduce-scatter.16.cloned.1.call-done = f32[80,2048]{1,0:T(8,128)} async-done(((f32[2560,2048]{1,0:T(8,128)}), f32[80,2048]{1,0:T(8,128)}) %reduce-scatter.16.cloned.1.call-update) | async-done | bytes 655376 | tf_op jit(solution)/shard_map/reduce_scatter | solution.py:287
  3008.6 442.5 %reduce-scatter.20.cloned.1.call-done = f32[192,2048]{1,0:T(8,128)} async-done(((f32[6144,2048]{1,0:T(8,128)}), f32[192,2048]{1,0:T(8,128)}) %reduce-scatter.20.cloned.1.call-update) | async-done | bytes 1572880 | tf_op jit(solution)/shard_map/reduce_scatter | solution.py:324
  (704 shorter events, 615.3 us)
Async XLA Ops:
  7.3 187.2 %all-gather.11.cloned.1.call-start = ((), (), s32[]{:S(2)}) async-start(), calls=%async_computation.7 | async-start | bytes 10813440 | tf_op jit(solution)/shard_map/all_gather | solution.py:102
  8.0 482.6 %all-gather.13.cloned.1.call-start = ((), (), s32[]{:S(2)}) async-start(), calls=%async_computation.8 | async-start | bytes 10813440 | tf_op jit(solution)/shard_map/all_gather | solution.py:101
  8.8 494.3 %all-gather.15.cloned.1.call-start = ((), (), s32[]{:S(2)}) async-start(), calls=%async_computation.9 | async-start | bytes 10813440 | tf_op jit(solution)/shard_map/all_gather | solution.py:110
  9.5 137.0 %copy-start.102 = (bf16[80,160]{1,0:T(8,128)(2,1)S(1)}, bf16[80,160]{1,0:T(8,128)(2,1)}, u32[]{:S(2)}) copy-start(bf16[80,160]{1,0:T(8,128)(2,1)} %param.32) | copy-start | bytes 76804
  9.5 500.0 %all-gather.19.cloned.1.call-start = ((), (), s32[]{:S(2)}) async-start(), calls=%async_computation.11 | async-start | bytes 25952256 | tf_op jit(solution)/shard_map/all_gather | solution.py:115
  10.1 594.1 %all-gather.17.cloned.1.call-start = ((), (), s32[]{:S(2)}) async-start(), calls=%async_computation.10 | async-start | bytes 25952256 | tf_op jit(solution)/shard_map/all_gather | solution.py:114
  10.7 749.1 %all-gather.21.cloned.1.call-start = ((), (), s32[]{:S(2)}) async-start(), calls=%async_computation.12 | async-start | bytes 25952256 | tf_op jit(solution)/shard_map/all_gather | solution.py:116
  11.3 1374.5 %reduce-scatter.22.cloned.1.call-start = ((), (), s32[]{:S(2)}) async-start(), calls=%async_computation.19 | async-start | bytes 1351680
  57.2 433.5 %copy-start.56 = (f32[2048]{0:T(1024)}, f32[2048]{0:T(1024)S(1)}, u32[]{:S(2)}) copy-start(f32[2048]{0:T(1024)S(1)} %convert_element_type.107) | copy-start | bytes 24580
  98.4 129.3 %copy-start.111 = (f32[256]{0:T(256)}, f32[256]{0:T(256)S(1)}, u32[]{:S(2)}) copy-start(f32[256]{0:T(256)S(1)} %subtract_convert_fusion) | copy-start | bytes 3076
  98.4 392.3 %copy-start.76 = (f32[256]{0:T(256)}, f32[256]{0:T(256)S(1)}, u32[]{:S(2)}) copy-start(f32[256]{0:T(256)S(1)} %fusion.70) | copy-start | bytes 3076
  100.2 127.4 %copy-start.81 = (f32[256]{0:T(256)}, f32[256]{0:T(256)S(1)}, u32[]{:S(2)}) copy-start(f32[256]{0:T(256)S(1)} %get-tuple-element.293) | copy-start | bytes 3076
  100.2 127.4 %copy-start.83 = (f32[256]{0:T(256)}, f32[256]{0:T(256)S(1)}, u32[]{:S(2)}) copy-start(f32[256]{0:T(256)S(1)} %get-tuple-element.294) | copy-start | bytes 3076
  100.2 127.4 %copy-start.85 = (f32[256]{0:T(256)}, f32[256]{0:T(256)S(1)}, u32[]{:S(2)}) copy-start(f32[256]{0:T(256)S(1)} %get-tuple-element.295) | copy-start | bytes 3076
  100.3 127.4 %copy-start.68 = (f32[2560]{0:T(1024)}, f32[2560]{0:T(1024)S(1)}, u32[]{:S(2)}) copy-start(f32[2560]{0:T(1024)S(1)} %broadcast_multiply_fusion) | copy-start | bytes 30724
  202.9 3.1 collective-permute-start
  509.2 301.8 %copy-start.26 = (f32[256,2048]{1,0:T(8,128)}, f32[256,2048]{1,0:T(8,128)S(1)}, u32[]{:S(2)}) copy-start(f32[256,2048]{1,0:T(8,128)S(1)} %get-tuple-element.298) | copy-start | bytes 6291460
  1098.8 570.9 %reduce-scatter.10.cloned.1.call-start = ((), (), s32[]{:S(2)}) async-start(), calls=%async_computation.13 | async-start | bytes 43253760 | tf_op jit(solution)/shard_map/reduce_scatter | solution.py:269
  1100.4 11.9 collective-permute-start.1
  1150.7 1358.0 %reduce-scatter.18.cloned.1.call-start = ((), (), s32[]{:S(2)}) async-start(), calls=%async_computation.17 | async-start | bytes 103809024 | tf_op jit(solution)/shard_map/reduce_scatter | solution.py:305
  1261.3 1387.0 %reduce-scatter.12.cloned.1.call-start = ((), (), s32[]{:S(2)}) async-start(), calls=%async_computation.14 | async-start | bytes 2703360 | tf_op jit(solution)/shard_map/reduce_scatter | solution.py:297
  1265.1 1519.6 %reduce-scatter.14.cloned.1.call-start = ((), (), s32[]{:S(2)}) async-start(), calls=%async_computation.15 | async-start | bytes 2703360 | tf_op jit(solution)/shard_map/reduce_scatter | solution.py:299
  1268.5 1740.0 %reduce-scatter.16.cloned.1.call-start = ((), (), s32[]{:S(2)}) async-start(), calls=%async_computation.16 | async-start | bytes 21626880 | tf_op jit(solution)/shard_map/reduce_scatter | solution.py:287
  1280.4 2170.7 %reduce-scatter.20.cloned.1.call-start = ((), (), s32[]{:S(2)}) async-start(), calls=%async_computation.18 | async-start | bytes 51904512 | tf_op jit(solution)/shard_map/reduce_scatter | solution.py:324
  (116 other events, 1410.0 us)
Sparse Core Ops, SparseCore 0:
  11.0 90.8 all-gather.10
  104.8 93.4 all-gather.12
  201.2 87.8 all-gather.14
  291.9 156.4 all-gather.18
  451.1 153.0 all-gather.16
  607.0 152.8 all-gather.20
  1098.9 130.9 reduce-scatter.21
  1232.3 437.3 reduce-scatter.9
  1677.2 831.4 reduce-scatter.17
  2511.5 136.8 reduce-scatter.11
  2651.3 133.3 reduce-scatter.13
  2787.6 220.9 reduce-scatter.15
  3016.7 434.2 reduce-scatter.19
where the time goes:
time: 3470 us; the launch traced here: 3460 us
  waiting for transfers between devices  2280 us (66%)
  local copies, waits for them, and re-layouts  357 us (10%)
  blocking collectives  345 us (10%)
  matrix products  256 us (7%)
  other arithmetic  195 us (6%)
    reduce_scatter x1, waiting for transfers between devices, on_device(): lax.psum_scatter(jnp.concatenate([lax.dot_general(columns, d_mlp_gate, co...  837 us
    reduce_scatter x1, waiting for transfers between devices, on_device(): lax.psum_scatter(lax.dot_general(columns, cotangent, contract_first, pref...  442 us
    reduce_scatter x1, waiting for transfers between devices, on_device(): lax.psum_scatter(jnp.concatenate([lax.dot_general(columns, d_gate_pre, co...  282 us
    reduce_scatter x1, waiting for transfers between devices, on_device(): lax.psum_scatter(lax.dot_general(columns, d_rec_out, contract_first, pref...  224 us
    all_gather x1, waiting for transfers between devices, on_device(): lax.all_gather(mlp_down_weight, ('wide', 'narrow'), axis=0, tiled=True)  141 us
    reduce_scatter x1, waiting for transfers between devices, on_device(): lax.psum_scatter(grad_input_whole, ('wide', 'narrow'), scatter_dimension=...  136 us
    reduce_scatter x1, waiting for transfers between devices, on_device(): lax.psum_scatter(grad_decay_whole, ('wide', 'narrow'), scatter_dimension=...  136 us
    all_gather x3, blocking collectives, carried_in(): gathered = jax.tree.map(lambda a: lax.all_gather(a, axis), part)  120 us
  transfers between devices with their start and end apart: 15, of which 8 were waited for; matrix products, arithmetic and copies ran while one was open for 14% of the time, Pallas kernels for 0%

commit v1 on v0

--- a/solution.py
+++ b/solution.py
@@ -11,6 +11,27 @@
 push_shift = 0.05
 contract_last = (((1,), (1,)), ((), ()))
 contract_first = (((0,), (0,)), ((), ()))
+
+
+def laid_out(blocks, dim):
+    dims = list(blocks.shape[1:])
+    dims[dim] *= blocks.shape[0]
+    return jnp.moveaxis(blocks, 0, dim).reshape(dims)
+
+
+def grow_blocks(shard, axis):
+    peers, mine = (lax.axis_size(axis), lax.axis_index(axis))
+    pieces, bit = (shard[None], 1)
+    while bit < peers:
+        theirs = lax.ppermute(pieces, axis, [(i, i ^ bit) for i in range(peers)])
+        low = mine & bit == 0
+        pieces = jnp.concatenate([jnp.where(low, pieces, theirs), jnp.where(low, theirs, pieces)])
+        bit *= 2
+    return pieces
+
+
+def doubled_up(x, axis, dim):
+    return laid_out(grow_blocks(x, axis), dim)
 
 
 def shifted(block, axis, distance):
@@ -111,7 +132,7 @@
     )
     mlp_set = (
         lax.all_gather(norm2_gain, ("wide", "narrow"), axis=0, tiled=True),
-        lax.all_gather(mlp_gate_weight, ("wide", "narrow"), axis=0, tiled=True),
+        doubled_up(mlp_gate_weight, ("wide", "narrow"), 0),
         lax.all_gather(mlp_up_weight, ("wide", "narrow"), axis=0, tiled=True),
         lax.all_gather(mlp_down_weight, ("wide", "narrow"), axis=0, tiled=True),
     )

time: 3470 us -> 4130 us (1.19)
  blocking collectives: 345 us -> 973 us
  waiting for transfers between devices: 2280 us -> 2190 us
  other arithmetic: 195 us -> 271 us
    all_gather x3, blocking collectives: 120 us -> 552 us  [carried_in(): gathered = jax.tree.map(lambda a: lax.all_gather(a, axis), part)]
    unnamed x2, blocking collectives: 90.2 us -> 284 us
    all_gather x1, waiting for transfers between devices: 141 us -> 0.01 us  [on_device(): lax.all_gather(mlp_down_weight, ('wide', 'narrow'), axis=0, tiled=True)]
    ppermute x0 -> x5, waiting for transfers between devices: none -> 133 us  [grow_blocks(): theirs = lax.ppermute(pieces, axis, [(i, i ^ bit) for i in range(peers)])]
    all_gather x1 -> x0, waiting for transfers between devices: 79.6 us -> none  [on_device(): lax.all_gather(mlp_gate_weight, ('wide', 'narrow'), axis=0, tiled=True)]
  transfers between devices with their start and end apart: 15 -> 19, of which waited for: 8 -> 9; matrix products, arithmetic and copies ran while one was open for 14% -> 14% of each run, Pallas kernels for 0% -> 0%
where the time goes in v1:
time: 4130 us; the launch traced here: 4110 us
  waiting for transfers between devices  2190 us (53%)
  blocking collectives  973 us (24%)
  local copies, waits for them, and re-layouts  393 us (10%)
  other arithmetic  271 us (7%)
  matrix products  253 us (6%)
    reduce_scatter x1, waiting for transfers between devices, on_device(): lax.psum_scatter(jnp.concatenate([lax.dot_general(columns, d_mlp_gate, co...  837 us
    all_gather x3, blocking collectives, carried_in(): gathered = jax.tree.map(lambda a: lax.all_gather(a, axis), part)  552 us
    reduce_scatter x1, waiting for transfers between devices, on_device(): lax.psum_scatter(lax.dot_general(columns, cotangent, contract_first, pref...  442 us
    unnamed x2, blocking collectives  284 us
    reduce_scatter x1, waiting for transfers between devices, on_device(): lax.psum_scatter(jnp.concatenate([lax.dot_general(columns, d_gate_pre, co...  283 us
    reduce_scatter x1, waiting for transfers between devices, on_device(): lax.psum_scatter(lax.dot_general(columns, d_rec_out, contract_first, pref...  224 us
    reduce_scatter x1, waiting for transfers between devices, on_device(): lax.psum_scatter(grad_input_whole, ('wide', 'narrow'), scatter_dimension=...  136 us
    reduce_scatter x1, waiting for transfers between devices, on_device(): lax.psum_scatter(grad_decay_whole, ('wide', 'narrow'), scatter_dimension=...  136 us
  transfers between devices with their start and end apart: 19, of which 9 were waited for; matrix products, arithmetic and copies ran while one was open for 14% of the time, Pallas kernels for 0%

profile of v1, /device:TPU:0, one launch (start us, length us, event | category | flops | bytes accessed | tf_op | source)
XLA Modules:
  0.0 4114.2 jit_solution(14138634074134535272)
XLA Ops:
  18.0 41.8 %collective-permute-done.2 = bf16[2,64,6144]{2,1,0:T(8,128)(2,1)} collective-permute-done((bf16[2,64,6144]{2,1,0:T(8,128)(2,1)S(1)}, bf16[2,64,6144]{2,1,0:T(8,128)(2,1)}, u32[]{:S(2)}, u32[]{:S(2)}) %collective-permute-start.2) | collective-permute-done | bytes 1572896 | tf_op jit(solution)/shard_map/ppermute | solution.py:26
  65.6 89.5 %collective-permute-done.3 = bf16[4,64,6144]{2,1,0:T(8,128)(2,1)} collective-permute-done((bf16[4,64,6144]{2,1,0:T(8,128)(2,1)}, bf16[4,64,6144]{2,1,0:T(8,128)(2,1)}, u32[]{:S(2)}, u32[]{:S(2)}) %collective-permute-start.3) | collective-permute-done | bytes 3145760 | tf_op jit(solution)/shard_map/ppermute | solution.py:26
  166.0 238.2 %all-reduce.88 = (bf16[2048]{0:T(1024)(128)(2,1)S(1)}, bf16[2560]{0:T(1024)(128)(2,1)S(1)}, bf16[2560]{0:T(1024)(128)(2,1)S(1)}, bf16[2560]{0:T(1024)(128)(2,1)S...) all-reduce(bf16[2048]{0:T(1024)(128)(2,1)S(1)} %dynamic-update-slic, ...), channel_id=1, replica_groups=mesh['wide'=8,'narrow'=4] {'wide','narrow'}, use_global_device_ids=true, to_apply=%add.76 | all-reduce | flops 14336 | bytes 57344
  405.4 39.6 all-gather
  447.3 48.4 %all_gather.57 = bf16[2560,160]{1,0:T(8,128)(2,1)} all-gather(bf16[80,160]{1,0:T(8,128)(2,1)S(1)} %copy-done.112), channel_id=1, replica_groups=mesh['wide'=8,'narrow'=4] {'wide','narrow'}, dimensions={0}, use_global_device_ids=true | all-gather | bytes 844800 | tf_op jit(solution)/shard_map/all_gather | solution.py:126
  495.7 49.9 %all_gather.61 = bf16[2560,160]{1,0:T(8,128)(2,1)} all-gather(bf16[80,160]{1,0:T(8,128)(2,1)S(1)} %copy-done.113), channel_id=1, replica_groups=mesh['wide'=8,'narrow'=4] {'wide','narrow'}, dimensions={0}, use_global_device_ids=true | all-gather | bytes 844800 | tf_op jit(solution)/shard_map/all_gather | solution.py:128
  774.6 111.6 %all-gather.1 = f32[32,1,2560]{2,1,0:T(1,128)S(1)} all-gather(f32[1,1,2560]{2,1,0:T(1,128)S(1)} %add_bitcast_fusion.1), channel_id=1, replica_groups=mesh['wide'=8,'narrow'=4] {'wide','narrow'}, dimensions={0}, use_global_device_ids=true | all-gather | bytes 337920 | tf_op jit(solution)/shard_map/all_gather | solution.py:47
  903.2 400.9 %all-gather.2 = f32[32,1,2560]{2,1,0:T(1,128)S(1)} all-gather(f32[1,1,2560]{2,1,0:T(1,128)S(1)} %add_bitcast_fusion), channel_id=1, replica_groups=mesh['wide'=8,'narrow'=4] {'wide','narrow'}, dimensions={0}, use_global_device_ids=true | all-gather | bytes 337920 | tf_op jit(solution)/shard_map/all_gather | solution.py:47
  1417.4 21.0 fusion.6
  1602.1 39.6 all-gather.3
  1641.8 30.6 while.27
  1689.8 21.0 rev.9
  1779.6 27.8 pad_maximum_fusion.1
  1808.6 21.3 fusion.109
  1830.0 21.4 fusion.110
  1851.3 67.1 %pad_maximum_fusion = f32[2048,12288]{1,0:T(8,128)} fusion(f32[2048,6144]{1,0:T(8,128)} %fusion.110, f32[2048,6144]{1,0:T(8,128)} %fusion.109), kind=kLoop, calls=%fused_computation.6 | loop fusion | flops 25165824 | bytes 201326592 | tf_op jit(solution)/shard_map/concatenate | solution.py:327
  1938.8 21.8 fusion.111
  1989.0 45.3 %all-reduce.87 = (f32[2048]{0:T(1024)S(1)}, f32[2560]{0:T(1024)S(1)}, f32[2560]{0:T(1024)S(1)}, f32[2560]{0:T(1024)S(1)}, f32[2560]{0:T(1024)S(1)}, /*index=5*/f32[2048]{0:T(1024)S(1)}) all-reduce(f32[2048]{0:T(1024)S(1)} %get-tuple-element.153, ...), channel_id=2, replica_groups=mesh['wide'=8,'narrow'=4] {'wide','narrow'}, use_global_device_ids=true, to_apply=%region_11.12.clone | all-reduce | flops 14336 | bytes 114688
  2042.8 283.5 %reduce-scatter.10.cloned.1.call-done = f32[64,5120]{1,0:T(8,128)} async-done(((f32[2048,5120]{1,0:T(8,128)}), f32[64,5120]{1,0:T(8,128)}) %reduce-scatter.10.cloned.1.call-update) | async-done | bytes 1310736 | tf_op jit(solution)/shard_map/reduce_scatter | solution.py:290
  2328.7 836.6 %reduce-scatter.18.cloned.1.call-done = f32[64,12288]{1,0:T(8,128)} async-done(((f32[2048,12288]{1,0:T(8,128)}), f32[64,12288]{1,0:T(8,128)}) %reduce-scatter.18.cloned.1.call-update) | async-done | bytes 3145744 | tf_op jit(solution)/shard_map/reduce_scatter | solution.py:326
  3169.1 135.5 %reduce-scatter.12.cloned.1.call-done = f32[80,160]{1,0:T(8,128)} async-done(((f32[2560,160]{1,0:T(8,128)}), f32[80,160]{1,0:T(8,128)}) %reduce-scatter.12.cloned.1.call-update) | async-done | bytes 51216 | tf_op jit(solution)/shard_map/reduce_scatter | solution.py:318
  3304.7 136.1 %reduce-scatter.14.cloned.1.call-done = f32[80,160]{1,0:T(8,128)} async-done(((f32[2560,160]{1,0:T(8,128)}), f32[80,160]{1,0:T(8,128)}) %reduce-scatter.14.cloned.1.call-update) | async-done | bytes 51216 | tf_op jit(solution)/shard_map/reduce_scatter | solution.py:320
  3440.8 224.0 %reduce-scatter.16.cloned.1.call-done = f32[80,2048]{1,0:T(8,128)} async-done(((f32[2560,2048]{1,0:T(8,128)}), f32[80,2048]{1,0:T(8,128)}) %reduce-scatter.16.cloned.1.call-update) | async-done | bytes 655376 | tf_op jit(solution)/shard_map/reduce_scatter | solution.py:308
  3664.9 442.3 %reduce-scatter.20.cloned.1.call-done = f32[192,2048]{1,0:T(8,128)} async-done(((f32[6144,2048]{1,0:T(8,128)}), f32[192,2048]{1,0:T(8,128)}) %reduce-scatter.20.cloned.1.call-update) | async-done | bytes 1572880 | tf_op jit(solution)/shard_map/reduce_scatter | solution.py:345
  (753 shorter events, 732.2 us)
Async XLA Ops:
  7.2 547.3 %all-gather.10.cloned.1.call-start = ((), (), s32[]{:S(2)}) async-start(), calls=%async_computation.7 | async-start | bytes 10813440 | tf_op jit(solution)/shard_map/all_gather | solution.py:123
  7.9 1325.4 %all-gather.12.cloned.1.call-start = ((), (), s32[]{:S(2)}) async-start(), calls=%async_computation.8 | async-start | bytes 10813440 | tf_op jit(solution)/shard_map/all_gather | solution.py:122
  8.7 1336.9 %all-gather.14.cloned.1.call-start = ((), (), s32[]{:S(2)}) async-start(), calls=%async_computation.9 | async-start | bytes 10813440 | tf_op jit(solution)/shard_map/all_gather | solution.py:131
  9.4 1380.0 %all-gather.16.cloned.1.call-start = ((), (), s32[]{:S(2)}) async-start(), calls=%async_computation.10 | async-start | bytes 25952256 | tf_op jit(solution)/shard_map/all_gather | solution.py:136
  10.0 1393.8 %all-gather.18.cloned.1.call-start = ((), (), s32[]{:S(2)}) async-start(), calls=%async_computation.11 | async-start | bytes 25952256 | tf_op jit(solution)/shard_map/all_gather | solution.py:137
  10.0 2.6 collective-permute-start.1
  15.1 44.7 %collective-permute-start.2 = (bf16[2,64,6144]{2,1,0:T(8,128)(2,1)S(1)}, bf16[2,64,6144]{2,1,0:T(8,128)(2,1)}, u32[]{:S(2)}, u32[]{:S(2)}) collective-permute-start(bf16[2,64,6144]{2,1,0:T(8,128)(2,1)S(1)} %pad_maximum_fusion.6), channel_id=1, source_target_pairs={{0,2},{1,3},{2,0},{3,1},{4,6},{5,7},{6,4},{7,5},{8,10},{9,11},{10,... | collective-permute-start | bytes 4718600 | tf_op jit(solution)/shard_map/ppermute | solution.py:26
  18.0 2023.4 %reduce-scatter.22.cloned.1.call-start = ((), (), s32[]{:S(2)}) async-start(), calls=%async_computation.18 | async-start | bytes 1351680
  63.9 91.2 %collective-permute-start.3 = (bf16[4,64,6144]{2,1,0:T(8,128)(2,1)}, bf16[4,64,6144]{2,1,0:T(8,128)(2,1)}, u32[]{:S(2)}, u32[]{:S(2)}) collective-permute-start(bf16[4,64,6144]{2,1,0:T(8,128)(2,1)} %pad_maximum_fusion.5), channel_id=1, source_target_pairs={{0,4},{1,5},{2,6},{3,7},{4,0},{5,1},{6,2},{7,3},{8,12},{9,13},{10,... | collective-permute-start | bytes 9437192 | tf_op jit(solution)/shard_map/ppermute | solution.py:26
  157.3 290.0 %copy-start.112 = (bf16[80,160]{1,0:T(8,128)(2,1)S(1)}, bf16[80,160]{1,0:T(8,128)(2,1)}, u32[]{:S(2)}) copy-start(bf16[80,160]{1,0:T(8,128)(2,1)} %param.30) | copy-start | bytes 76804
  161.9 333.8 %copy-start.113 = (bf16[80,160]{1,0:T(8,128)(2,1)S(1)}, bf16[80,160]{1,0:T(8,128)(2,1)}, u32[]{:S(2)}) copy-start(bf16[80,160]{1,0:T(8,128)(2,1)} %param.32) | copy-start | bytes 76804
  161.9 383.7 %collective-permute-start.4 = (bf16[8,64,6144]{2,1,0:T(8,128)(2,1)}, bf16[8,64,6144]{2,1,0:T(8,128)(2,1)}, u32[]{:S(2)}, u32[]{:S(2)}) collective-permute-start(bf16[8,64,6144]{2,1,0:T(8,128)(2,1)} %pad_maximum_fusion.4), channel_id=1, source_target_pairs={{0,8},{1,9},{2,10},{3,11},{4,12},{5,13},{6,14},{7,15},{8,0},{9,1},... | collective-permute-start | bytes 18874376 | tf_op jit(solution)/shard_map/ppermute | solution.py:26
  404.2 929.1 %copy-start.59 = (f32[2048]{0:T(1024)}, f32[2048]{0:T(1024)S(1)}, u32[]{:S(2)}) copy-start(f32[2048]{0:T(1024)S(1)} %convert_element_type.107) | copy-start | bytes 24580
  445.7 887.6 %copy-start.83 = (f32[256]{0:T(256)}, f32[256]{0:T(256)S(1)}, u32[]{:S(2)}) copy-start(f32[256]{0:T(256)S(1)} %fusion.70) | copy-start | bytes 3076
  561.6 8.5 collective-permute-start
  570.1 782.1 %collective-permute-start.5 = (bf16[16,64,6144]{2,1,0:T(8,128)(2,1)}, bf16[16,64,6144]{2,1,0:T(8,128)(2,1)}, u32[]{:S(2)}, u32[]{:S(2)}) collective-permute-start(bf16[16,64,6144]{2,1,0:T(8,128)(2,1)} %pad_maximum_fusion.3), channel_id=1, source_target_pairs={{0,16},{1,17},{2,18},{3,19},{4,20},{5,21},{6,22},{7,23},{8,24},{9,... | collective-permute-start | bytes 37748744 | tf_op jit(solution)/shard_map/ppermute | solution.py:26
  902.2 402.6 %copy-start.27 = (f32[256,2560]{1,0:T(8,128)}, f32[256,2560]{1,0:T(8,128)S(1)}, u32[]{:S(2)}) copy-start(f32[256,2560]{1,0:T(8,128)S(1)} %pad.254) | copy-start | bytes 7864324
  1755.4 570.9 %reduce-scatter.10.cloned.1.call-start = ((), (), s32[]{:S(2)}) async-start(), calls=%async_computation.12 | async-start | bytes 43253760 | tf_op jit(solution)/shard_map/reduce_scatter | solution.py:290
  1757.2 11.9 collective-permute-start.6
  1807.4 1357.9 %reduce-scatter.18.cloned.1.call-start = ((), (), s32[]{:S(2)}) async-start(), calls=%async_computation.16 | async-start | bytes 103809024 | tf_op jit(solution)/shard_map/reduce_scatter | solution.py:326
  1918.5 1386.1 %reduce-scatter.12.cloned.1.call-start = ((), (), s32[]{:S(2)}) async-start(), calls=%async_computation.13 | async-start | bytes 2703360 | tf_op jit(solution)/shard_map/reduce_scatter | solution.py:318
  1922.3 1518.6 %reduce-scatter.14.cloned.1.call-start = ((), (), s32[]{:S(2)}) async-start(), calls=%async_computation.14 | async-start | bytes 2703360 | tf_op jit(solution)/shard_map/reduce_scatter | solution.py:320
  1925.6 1739.2 %reduce-scatter.16.cloned.1.call-start = ((), (), s32[]{:S(2)}) async-start(), calls=%async_computation.15 | async-start | bytes 21626880 | tf_op jit(solution)/shard_map/reduce_scatter | solution.py:308
  1937.6 2169.6 %reduce-scatter.20.cloned.1.call-start = ((), (), s32[]{:S(2)}) async-start(), calls=%async_computation.17 | async-start | bytes 51904512 | tf_op jit(solution)/shard_map/reduce_scatter | solution.py:345
  (135 other events, 3793.6 us)
Sparse Core Ops, SparseCore 0:
  10.9 112.0 all-gather.9
  125.9 113.1 all-gather.11
  242.0 128.4 all-gather.13
  373.3 176.6 all-gather.15
  552.7 480.9 all-gather.17
  1755.5 130.9 reduce-scatter.21
  1888.9 437.3 reduce-scatter.9
  2333.8 831.4 reduce-scatter.17
  3168.2 136.3 reduce-scatter.11
  3307.5 133.3 reduce-scatter.13
  3443.8 221.0 reduce-scatter.15
  3672.8 434.2 reduce-scatter.19
